TPU v7x, 256 devices: a whole 4x4x8 slice. The times are simulated.
256 devices in a mesh: pts: 64 (over z, x, core), blk: 4 (over y).
Axes of the slice: x: 4, y: 4, z: 8, core: 2. Of those that a mesh axis runs over, the one named last changes fastest.
Arguments:
- points: bfloat16 [2097152, 128], P(('pts', 'blk')), may hold values from -1.5 to 1.5
- targets: float32 [2097152, 64], P(('pts', 'blk')), may hold values from -6 to 6
- coefs: float32 [2097152, 64], P(('pts', 'blk')), may hold values from -0.5 to 0.5
- preds: float32 [2097152, 64], P(('pts', 'blk')), may hold values from -32 to 32
- block_inverse: float32 [2048, 2048], P('blk'), may hold values from -0.2 to 2.2
- block_id: int32 [1], replicated, may hold values from 0 to 1023
Outputs:
- new_coefs: float32 [2097152, 64], P(('pts', 'blk'))
- new_preds: float32 [2097152, 64], P(('pts', 'blk'))
All inputs are finite; a program needn't handle non-finite values.
Results may differ from a plain program's by a relative error of at most 0.0042.
Values may be sent and summed in bfloat16 or wider, within the bound.
A program may use at most 128 MiB of HBM per device.

v0:
```python
import jax
import jax.numpy as jnp
from jax import lax
from jax.sharding import Mesh
from jax.sharding import PartitionSpec as P

PTS_BLK = ("pts_0", "pts_1", "pts_2", "blk")
damping = 1.0
inverse_width = 0.25


def spread(value, axes, root):
    value = jnp.where(lax.axis_index(axes) == root, value, jnp.zeros_like(value))
    for axis in axes:
        value = lax.psum(value, axis)
    return value


def in_blocks(value, dim, length):
    before, after = (value.shape[:dim], value.shape[dim + 1 :])
    return jnp.moveaxis(value.reshape(*before, length, -1, *after), dim, 0)


def sum_at_owner(value, axis, dim):
    pieces = in_blocks(value, dim, lax.axis_size(axis))
    arrived = lax.all_to_all(pieces, axis, split_axis=0, concat_axis=0, tiled=True)
    return arrived.sum(axis=0)


def summed_rows(value, axes, dim):
    far, near = axes
    pieces = in_blocks(value, dim, lax.axis_size(far))
    nearer = sum_at_owner(pieces, near, dim + 1)
    arrived = lax.all_to_all(nearer, far, split_axis=0, concat_axis=0, tiled=True)
    return arrived.sum(axis=0)


def filled_up(lines, length):
    spare = -len(lines) % length
    return jnp.pad(lines, [(0, spare)] + [(0, 0)] * (lines.ndim - 1))


def from_everyone(value, axis):
    copies = jnp.broadcast_to(value, (lax.axis_size(axis), *value.shape))
    return lax.all_to_all(copies, axis, split_axis=0, concat_axis=0, tiled=True)


def laid_out(pieces, dim):
    pieces = jnp.moveaxis(pieces, 0, dim)
    lengths = pieces.shape
    return pieces.reshape(*lengths[:dim], lengths[dim] * lengths[dim + 1], *lengths[dim + 2 :])


def gather_axes(value, axes, dim):
    far, near = axes
    pieces = from_everyone(from_everyone(value, far), near)
    return laid_out(pieces.swapaxes(0, 1).reshape(-1, *value.shape), dim)


def total_of(value, axes):
    lines = value.reshape(-1, value.shape[-1])
    own = summed_rows(filled_up(lines, lax.axis_size(axes[0]) * lax.axis_size(axes[1])), axes, 0)
    whole = gather_axes(own, axes, 0)
    return whole[: len(lines)].reshape(value.shape)


def gathered_copies(value, axis, dim):
    return laid_out(from_everyone(value, axis), dim)


def kernel_rows(centers, others):
    center_wide = centers.astype(jnp.float32)
    other_wide = others.astype(jnp.float32)
    center_squares = jnp.sum(center_wide * center_wide, axis=1)
    point_squares = jnp.sum(other_wide * other_wide, axis=1)
    inner_products = jnp.dot(centers, others.T, preferred_element_type=jnp.float32)
    distance = center_squares[:, None] + point_squares[None, :] - 2.0 * inner_products
    return jnp.exp(-inverse_width * distance).astype(jnp.bfloat16)


def body(points, targets, coefs, preds, block_inverse, block_id):
    shard_rows = points.shape[0]
    block_order = block_inverse.shape[1]
    targets_width = targets.shape[1]
    block_start = block_id[0] * block_order
    owner_index = block_start // shard_rows
    offset = block_start % shard_rows
    is_owner = lax.axis_index(PTS_BLK) == owner_index
    local_centers = lax.dynamic_slice_in_dim(points, offset, block_order, 0)
    centers = spread(local_centers, PTS_BLK, owner_index)
    tile_width = min(512, shard_rows)
    tile_count = shard_rows // tile_width
    point_tiles = points.reshape(tile_count, tile_width, points.shape[1])
    coef_tiles = coefs.astype(jnp.bfloat16).reshape(tile_count, tile_width, targets_width)
    kernel = lax.map(lambda tile_points: kernel_rows(centers, tile_points), point_tiles)
    summed = jnp.einsum("nbs,nsd->bd", kernel, coef_tiles, preferred_element_type=jnp.float32)
    block_coefs = lax.dynamic_slice_in_dim(coefs, offset, block_order, 0)
    own_block = lax.dynamic_slice_in_dim(targets, offset, block_order, 0) - damping * block_coefs
    own_term = jnp.where(is_owner, own_block, 0.0) - summed
    slab_part = sum_at_owner(own_term, "blk", 0)
    slab_part = total_of(slab_part, (("pts_0", "pts_1"), "pts_2"))
    residual = gathered_copies(slab_part, "blk", 0)
    slab_update = jnp.dot(block_inverse, residual, precision=lax.Precision.HIGHEST)
    update = gathered_copies(slab_update, "blk", 0)
    new_coefs = jnp.where(
        is_owner, lax.dynamic_update_slice_in_dim(coefs, block_coefs + update, offset, 0), coefs
    )
    update_half = update.astype(jnp.bfloat16)
    shifts = jnp.einsum("nbs,bd->nsd", kernel, update_half, preferred_element_type=jnp.float32)
    new_preds = preds + shifts.reshape(shard_rows, targets_width)
    return (new_coefs, new_preds)


def solution(mesh):
    split = Mesh(
        mesh.devices.reshape(8, 4, 2, mesh.shape["blk"]), ("pts_0", "pts_1", "pts_2", "blk")
    )
    in_specs = (
        P(PTS_BLK, None),
        P(PTS_BLK, None),
        P(PTS_BLK, None),
        P(PTS_BLK, None),
        P("blk", None),
        P(),
    )
    out_specs = (P(PTS_BLK, None), P(PTS_BLK, None))
    return jax.shard_map(body, mesh=split, in_specs=in_specs, out_specs=out_specs, check_vma=False)
```

profile of v0, /device:TPU:1, one launch (start us, length us, event | category | flops | bytes accessed | tf_op | source)
XLA Modules:
  0.0 446.5 jit_solution(14518260487018970397)
XLA Ops:
  7.2 1.6 copy.69
  9.5 2.0 dynamic-slice_select_fusion
  11.6 73.0 %all-reduce.5.cloned.1.call-done = bf16[2048,128]{1,0:T(8,128)(2,1)} async-done(((bf16[2048,128]{1,0:T(8,128)(2,1)}), bf16[2048,128]{1,0:T(8,128)(2,1)}) %all-reduce.5.cloned.1.call-update) | async-done | bytes 524304 | tf_op jit(solution)/shard_map/psum | solution.py:15
  84.6 51.3 %all-reduce.7.cloned.1.call-done = bf16[2048,128]{1,0:T(8,128)(2,1)} async-done(((bf16[2048,128]{1,0:T(8,128)(2,1)}), bf16[2048,128]{1,0:T(8,128)(2,1)}) %all-reduce.7.cloned.1.call-update) | async-done | bytes 524304 | tf_op jit(solution)/shard_map/psum | solution.py:15
  136.0 35.4 %all-reduce.9.cloned.1.call-done = bf16[2048,128]{1,0:T(8,128)(2,1)} async-done(((bf16[2048,128]{1,0:T(8,128)(2,1)}), bf16[2048,128]{1,0:T(8,128)(2,1)}) %all-reduce.9.cloned.1.call-update) | async-done | bytes 524304 | tf_op jit(solution)/shard_map/psum | solution.py:15
  171.6 48.7 %all-reduce.11.cloned.1.call-done = bf16[2048,128]{1,0:T(8,128)(2,1)} async-done(((bf16[2048,128]{1,0:T(8,128)(2,1)}), bf16[2048,128]{1,0:T(8,128)(2,1)}) %all-reduce.11.cloned.1.call-update) | async-done | bytes 524304 | tf_op jit(solution)/shard_map/psum | solution.py:15
  220.3 96.1 %while.10 = (s32[]{:T(128)}, bf16[16,2048,512]{1,2,0:T(8,128)(2,1)}, bf16[2048,128]{1,0:T(8,128)(2,1)}, bf16[16,512,128]{2,1,0:T(8,128)(2,1)}, s32[]{:T(128)}) while((s32[]{:T(128)}, bf16[16,2048,512]{1,2,0:T(8,128)(2,1)}, bf16[2048,128]{1,0:T(8,128)(2,1)}, bf16[16,512,128]{2,1,0:T(8,128)(2,1)}, s32[]{:T(128)}) %tuple.33), condition=%wide.region_7.8_spmd, body=%wide.region_4.7_spmd.sunk | while | flops 274658816 | bytes 3429441 | solution.py:95
  220.3 1.0 multiply_reduce_fusion.4
  221.3 1.4 multiply_reduce_fusion.5
  222.7 3.6 fusion.22
  226.3 1.0 multiply_reduce_fusion.4
  227.4 1.4 multiply_reduce_fusion.5
  228.8 3.5 fusion.22
  232.3 1.0 multiply_reduce_fusion.4
  233.3 1.4 multiply_reduce_fusion.5
  234.7 3.6 fusion.22
  238.3 1.0 multiply_reduce_fusion.4
  239.3 1.4 multiply_reduce_fusion.5
  240.7 3.6 fusion.22
  244.3 1.0 multiply_reduce_fusion.4
  245.3 1.4 multiply_reduce_fusion.5
  246.7 3.6 fusion.22
  250.3 1.0 multiply_reduce_fusion.4
  251.4 1.4 multiply_reduce_fusion.5
  252.8 3.5 fusion.22
  256.3 1.0 multiply_reduce_fusion.4
  257.4 1.4 multiply_reduce_fusion.5
  258.8 3.6 fusion.22
  262.3 1.0 multiply_reduce_fusion.4
  263.4 1.4 multiply_reduce_fusion.5
  264.8 3.6 fusion.22
  268.3 1.0 multiply_reduce_fusion.4
  269.4 1.4 multiply_reduce_fusion.5
  270.8 3.6 fusion.22
  274.4 1.0 multiply_reduce_fusion.4
  275.4 1.4 multiply_reduce_fusion.5
  276.8 3.5 fusion.22
  280.3 1.0 multiply_reduce_fusion.4
  281.4 1.4 multiply_reduce_fusion.5
  282.8 3.5 fusion.22
  286.3 1.0 multiply_reduce_fusion.4
  287.4 1.4 multiply_reduce_fusion.5
  288.8 3.6 fusion.22
  293.4 1.4 multiply_reduce_fusion.5
  294.8 3.6 fusion.22
  298.4 1.0 multiply_reduce_fusion.4
  299.4 1.4 multiply_reduce_fusion.5
  300.8 3.5 fusion.22
  304.3 1.0 multiply_reduce_fusion.4
  305.4 1.4 multiply_reduce_fusion.5
  306.8 3.6 fusion.22
  310.4 1.0 multiply_reduce_fusion.4
  311.4 1.4 multiply_reduce_fusion.5
  312.8 3.5 fusion.22
  316.3 14.1 %fusion.8 = f32[2048,64]{0,1:T(8,128)S(1)} fusion(bf16[16,2048,512]{1,2,0:T(8,128)(2,1)} %get-tuple-element.24, bf16[8,16,8,512]{3,2,1,0:T(8,128)(2,1)S(1)} %bitcast.68, f32[8192,64]{0,1:T(8,128)} %param.9, s32[]{:T(128)S(6)} %select_n.44, f32[8192,64]{0,1:T(8,128)S(1)} %copy.69, pred[]{:T(512)S(6)} %eq.6), kind=kOutput, calls=%fused_computation.13 | convolution fusion | flops 2147876864 | bytes 36175876 | tf_op jit(solution)/shard_map/nbs,nsd->bd/dot_general | solution.py:96
  330.5 10.2 %all_to_all.35 = f32[4,512,64]{1,2,0:T(8,128)S(1)} all-to-all(f32[4,512,64]{1,2,0:T(8,128)S(1)} %bitcast.72), channel_id=1, replica_groups=mesh['pts_0'=8,'pts_1'=4,'pts_2'=2,'blk'=4] {'blk'}, dimensions={0} | all-to-all | bytes 1048576 | tf_op jit(solution)/shard_map/all_to_all | solution.py:26
  341.1 7.7 %all_to_all.36 = f32[2,1,16384]{2,1,0:T(1,128)S(1)} all-to-all(f32[2,1,16384]{2,1,0:T(1,128)S(1)} %reshape.32), channel_id=1, replica_groups=mesh['pts_0'=8,'pts_1'=4,'pts_2'=2,'blk'=4] {'pts_2'}, dimensions={0} | all-to-all | bytes 262144 | tf_op jit(solution)/shard_map/all_to_all | solution.py:26
  350.7 18.1 %all_to_all.37 = f32[32,1,512]{2,1,0:T(1,128)S(1)} all-to-all(f32[32,1,512]{2,1,0:T(1,128)S(1)} %reshape.34), channel_id=1, replica_groups=mesh['pts_0'=8,'pts_1'=4,'pts_2'=2,'blk'=4] {'pts_0','pts_1'}, dimensions={0} | all-to-all | bytes 131072 | tf_op jit(solution)/shard_map/all_to_all | solution.py:34
  369.9 12.0 %all_to_all.38 = f32[32,1,512]{2,1,0:T(1,128)S(1)} all-to-all(f32[32,1,512]{2,1,0:T(1,128)S(1)} %reshape.36), channel_id=1, replica_groups=mesh['pts_0'=8,'pts_1'=4,'pts_2'=2,'blk'=4] {'pts_0','pts_1'}, dimensions={0} | all-to-all | bytes 131072 | tf_op jit(solution)/shard_map/all_to_all | solution.py:45
  383.0 6.4 %all_to_all.39 = f32[2,1,16384]{2,1,0:T(1,128)S(1)} all-to-all(f32[2,1,16384]{2,1,0:T(1,128)S(1)} %reshape.38), channel_id=1, replica_groups=mesh['pts_0'=8,'pts_1'=4,'pts_2'=2,'blk'=4] {'pts_2'}, dimensions={0} | all-to-all | bytes 262144 | tf_op jit(solution)/shard_map/all_to_all | solution.py:45
  390.8 11.6 %all_to_all.40 = f32[4,512,64]{1,2,0:T(8,128)S(1)} all-to-all(f32[4,512,64]{1,2,0:T(8,128)S(1)} %broadcast_in_dim.33), channel_id=1, replica_groups=mesh['pts_0'=8,'pts_1'=4,'pts_2'=2,'blk'=4] {'blk'}, dimensions={0} | all-to-all | bytes 1048576 | tf_op jit(solution)/shard_map/all_to_all | solution.py:45
  402.5 6.3 %convolution_bitcast_fusion.1 = f32[512,64]{0,1:T(8,128)S(1)} fusion(f32[2048,64]{0,1:T(8,128)S(1)} %bitcast.71, f32[512,2048]{1,0:T(8,128)} %param.12), kind=kOutput, calls=%fused_computation.14 | convolution fusion | flops 805306368 | bytes 4849664 | tf_op jit(solution)/shard_map/dot_general | solution.py:103
  408.8 10.9 %all_to_all.41 = f32[4,512,64]{1,2,0:T(8,128)S(1)} all-to-all(f32[4,512,64]{1,2,0:T(8,128)S(1)} %broadcast_in_dim.34), channel_id=1, replica_groups=mesh['pts_0'=8,'pts_1'=4,'pts_2'=2,'blk'=4] {'blk'}, dimensions={0} | all-to-all | bytes 1048576 | tf_op jit(solution)/shard_map/all_to_all | solution.py:45
  421.0 19.1 %convolution_add_fusion = f32[8192,64]{0,1:T(8,128)} fusion(f32[8192,64]{0,1:T(8,128)} %param.11, bf16[8192,2048]{1,0:T(8,128)(2,1)} %bitcast.67, bf16[2048,64]{0,1:T(8,128)(2,1)S(1)} %bitcast.75), kind=kOutput, calls=%fused_computation.11 | convolution fusion | flops 2148007936 | bytes 38010880 | tf_op jit(solution)/shard_map/nbs,bd->nsd/dot_general | solution.py:109
  (44 shorter events, 8.4 us)
Async XLA Ops:
  7.2 77.4 %all-reduce.5.cloned.1.call-start = ((), (), s32[]{:S(2)}) async-start(), calls=%async_computation.7 | async-start | bytes 1048576 | tf_op jit(solution)/shard_map/psum | solution.py:15
  11.5 124.4 %all-reduce.7.cloned.1.call-start = ((), (), s32[]{:S(2)}) async-start(), calls=%async_computation.8 | async-start | bytes 1048576 | tf_op jit(solution)/shard_map/psum | solution.py:15
  84.6 86.9 %all-reduce.9.cloned.1.call-start = ((), (), s32[]{:S(2)}) async-start(), calls=%async_computation.9 | async-start | bytes 1048576 | tf_op jit(solution)/shard_map/psum | solution.py:15
  136.0 84.3 %all-reduce.11.cloned.1.call-start = ((), (), s32[]{:S(2)}) async-start(), calls=%async_computation.10 | async-start | bytes 1048576 | tf_op jit(solution)/shard_map/psum | solution.py:15
  420.9 19.1 %copy-start = (f32[8192,64]{0,1:T(8,128)}, f32[8192,64]{0,1:T(8,128)S(1)}, u32[]{:S(2)}) copy-start(f32[8192,64]{0,1:T(8,128)S(1)} %select_n.49) | copy-start | bytes 6291460
Sparse Core Ops, SparseCore 0:
  11.7 72.8 all-reduce.4
  86.9 49.0 all-reduce.6
  138.6 32.8 all-reduce.8
  173.6 46.5 all-reduce.10
where the time goes:
time: 448 us; the launch traced here: 447 us
  waiting for transfers between devices  208 us (46%)
  matrix products  96.4 us (22%)
  blocking collectives  77 us (17%)
  other arithmetic  45.1 us (10%)
  between operations  14.7 us (3%)
  local copies, waits for them, and re-layouts  4.66 us (1%)
    psum x4, waiting for transfers between devices, spread(): value = lax.psum(value, axis)  208 us
    dot_general x16, matrix products, kernel_rows(): jnp.dot(centers, others.T, preferred_element_type=jnp.float32)  56.9 us
    all_to_all x4, blocking collectives, from_everyone(): return lax.all_to_all(copies, axis, split_axis=0, concat_axis=0, tiled=True)  41 us
    reduce_sum x16, other arithmetic, kernel_rows(): center_squares = jnp.sum(center_wide * center_wide, axis=1)  22.2 us
    dot_general x1, matrix products, body(): jnp.einsum('nbs,bd->nsd', kernel, update_half, preferred_element_type=jnp...  19.1 us
    all_to_all x1, blocking collectives, summed_rows(): lax.all_to_all(nearer, far, split_axis=0, concat_axis=0, tiled=True)  18.1 us
    all_to_all x2, blocking collectives, sum_at_owner(): lax.all_to_all(pieces, axis, split_axis=0, concat_axis=0, tiled=True)  17.9 us
    reduce_sum x16, other arithmetic, kernel_rows(): point_squares = jnp.sum(other_wide * other_wide, axis=1)  16.8 us
  transfers between devices with their start and end apart: 4, of which 4 were waited for; matrix products, arithmetic and copies ran while one was open for 0% of the time, Pallas kernels for 0%

commit v1 on v0

--- a/solution.py
+++ b/solution.py
@@ -12,7 +12,7 @@
 def spread(value, axes, root):
     value = jnp.where(lax.axis_index(axes) == root, value, jnp.zeros_like(value))
     for axis in axes:
-        value = lax.psum(value, axis)
+        value = jnp.sum(lax.all_gather(value, axis), axis=0)
     return value
 
 

time: 448 us -> 371 us (0.83)
  waiting for transfers between devices: 208 us -> 139 us
  other arithmetic: 45.1 us -> 40.4 us
    psum x4 -> x0, waiting for transfers between devices: 208 us -> none  [spread(): value = lax.psum(value, axis)]
    all_gather x0 -> x4, waiting for transfers between devices: none -> 139 us  [spread(): value = jnp.sum(lax.all_gather(value, axis), axis=0)]
    reduce_sum x16, other arithmetic: 22.2 us -> 5.5 us  [kernel_rows(): center_squares = jnp.sum(center_wide * center_wide, axis=1)]
    reduce_sum x0 -> x4, other arithmetic: none -> 11.1 us  [spread(): value = jnp.sum(lax.all_gather(value, axis), axis=0)]
where the time goes in v1:
time: 371 us; the launch traced here: 370 us
  waiting for transfers between devices  139 us (37%)
  matrix products  95.6 us (26%)
  blocking collectives  75.6 us (20%)
  other arithmetic  40.4 us (11%)
  between operations  14.7 us (4%)
  local copies, waits for them, and re-layouts  4.66 us (1%)
    all_gather x4, waiting for transfers between devices, spread(): value = jnp.sum(lax.all_gather(value, axis), axis=0)  139 us
    dot_general x16, matrix products, kernel_rows(): jnp.dot(centers, others.T, preferred_element_type=jnp.float32)  53.5 us
    all_to_all x4, blocking collectives, from_everyone(): return lax.all_to_all(copies, axis, split_axis=0, concat_axis=0, tiled=True)  41 us
    dot_general x1, matrix products, body(): jnp.einsum('nbs,bd->nsd', kernel, update_half, preferred_element_type=jnp...  19 us
    all_to_all x1, blocking collectives, summed_rows(): lax.all_to_all(nearer, far, split_axis=0, concat_axis=0, tiled=True)  18.2 us
    dot_general x1, matrix products, body(): jnp.einsum('nbs,nsd->bd', kernel, coef_tiles, preferred_element_type=jnp....  16.8 us
    reduce_sum x16, other arithmetic, kernel_rows(): point_squares = jnp.sum(other_wide * other_wide, axis=1)  16.8 us
    all_to_all x2, blocking collectives, sum_at_owner(): lax.all_to_all(pieces, axis, split_axis=0, concat_axis=0, tiled=True)  16.4 us
  transfers between devices with their start and end apart: 4, of which 4 were waited for; matrix products, arithmetic and copies ran while one was open for 0% of the time, Pallas kernels for 0%

profile of v1, /device:TPU:1, one launch (start us, length us, event | category | flops | bytes accessed | tf_op | source)
XLA Modules:
  0.0 370.1 jit_solution(4864867534452757038)
XLA Ops:
  7.2 1.6 copy.65
  9.5 2.0 dynamic-slice_select_fusion
  11.6 58.5 %all-gather.9.cloned.1.call-done = bf16[16384,128]{1,0:T(8,128)(2,1)} async-done(((bf16[2048,128]{1,0:T(8,128)(2,1)}), bf16[16384,128]{1,0:T(8,128)(2,1)}) %all-gather.9.cloned.1.call-update) | async-done | bytes 4194320 | tf_op jit(solution)/shard_map/all_gather | solution.py:15
  70.1 3.7 reduce_sum.93
  73.8 32.0 %all-gather.11.cloned.1.call-done = bf16[8192,128]{1,0:T(8,128)(2,1)} async-done(((bf16[2048,128]{1,0:T(8,128)(2,1)}), bf16[8192,128]{1,0:T(8,128)(2,1)}) %all-gather.11.cloned.1.call-update) | async-done | bytes 2097168 | tf_op jit(solution)/shard_map/all_gather | solution.py:15
  105.8 2.8 reduce_sum.94
  108.8 15.4 %all-gather.13.cloned.1.call-done = bf16[4096,128]{1,0:T(8,128)(2,1)} async-done(((bf16[2048,128]{1,0:T(8,128)(2,1)}), bf16[4096,128]{1,0:T(8,128)(2,1)}) %all-gather.13.cloned.1.call-update) | async-done | bytes 1048592 | tf_op jit(solution)/shard_map/all_gather | solution.py:15
  124.2 2.3 reduce_sum.95
  126.6 1.1 convert_element_type.26
  127.6 32.8 %all-gather.15.cloned.1.call-done = bf16[8192,128]{1,0:T(8,128)(2,1)} async-done(((bf16[2048,128]{1,0:T(8,128)(2,1)}), bf16[8192,128]{1,0:T(8,128)(2,1)}) %all-gather.15.cloned.1.call-update) | async-done | bytes 2097168 | tf_op jit(solution)/shard_map/all_gather | solution.py:15
  160.5 2.2 reduce_sum.96
  162.6 76.0 %while.10 = (s32[]{:T(128)}, bf16[16,2048,512]{1,2,0:T(8,128)(2,1)}, bf16[2048,128]{1,0:T(8,128)(2,1)S(1)}, bf16[16,512,128]{2,1,0:T(8,128)(2,1)}, s32[]{:T(128)}) while((s32[]{:T(128)}, bf16[16,2048,512]{1,2,0:T(8,128)(2,1)}, bf16[2048,128]{1,0:T(8,128)(2,1)S(1)}, bf16[16,512,128]{2,1,0:T(8,128)(2,1)}, s32[]{:T(128)}) %tuple.33), condition=%wide.region_7.8_spmd, body=%wide.region_4.7_spmd.sunk | while | flops 274658816 | bytes 3429441 | solution.py:95
  162.7 1.1 multiply_reduce_fusion.4
  163.7 0.3 multiply_reduce_fusion.5
  164.1 3.4 fusion.22
  167.4 1.0 multiply_reduce_fusion.4
  168.5 0.3 multiply_reduce_fusion.5
  168.8 3.3 fusion.22
  172.1 1.0 multiply_reduce_fusion.4
  173.5 3.3 fusion.22
  176.9 1.0 multiply_reduce_fusion.4
  178.3 3.4 fusion.22
  181.6 1.0 multiply_reduce_fusion.4
  183.0 3.4 fusion.22
  186.4 1.0 multiply_reduce_fusion.4
  187.8 3.3 fusion.22
  191.1 1.0 multiply_reduce_fusion.4
  192.5 3.4 fusion.22
  195.9 1.0 multiply_reduce_fusion.4
  197.3 3.3 fusion.22
  200.7 1.0 multiply_reduce_fusion.4
  202.1 3.4 fusion.22
  205.4 1.0 multiply_reduce_fusion.4
  206.8 3.3 fusion.22
  210.1 1.0 multiply_reduce_fusion.4
  211.5 3.3 fusion.22
  214.9 1.0 multiply_reduce_fusion.4
  216.3 3.4 fusion.22
  219.6 1.0 multiply_reduce_fusion.4
  220.7 0.3 multiply_reduce_fusion.5
  221.0 3.4 fusion.22
  224.4 1.0 multiply_reduce_fusion.4
  225.8 3.3 fusion.22
  229.1 1.0 multiply_reduce_fusion.4
  230.2 0.3 multiply_reduce_fusion.5
  230.5 3.4 fusion.22
  233.9 1.0 multiply_reduce_fusion.4
  235.3 3.3 fusion.22
  238.6 16.8 %fusion.8 = f32[2048,64]{0,1:T(8,128)S(1)} fusion(bf16[16,2048,512]{1,2,0:T(8,128)(2,1)} %get-tuple-element.24, bf16[8,16,8,512]{3,2,1,0:T(8,128)(2,1)} %bitcast.72, f32[8192,64]{0,1:T(8,128)} %param.9, s32[]{:T(128)S(6)} %select_n.44, f32[8192,64]{0,1:T(8,128)S(1)} %copy.65, pred[]{:T(512)S(6)} %eq.6), kind=kOutput, calls=%fused_computation.13 | convolution fusion | flops 2147876864 | bytes 36175876 | tf_op jit(solution)/shard_map/nbs,nsd->bd/dot_general | solution.py:96
  255.5 11.0 %all_to_all.35 = f32[4,512,64]{1,2,0:T(8,128)S(1)} all-to-all(f32[4,512,64]{1,2,0:T(8,128)S(1)} %bitcast.79), channel_id=1, replica_groups=mesh['pts_0'=8,'pts_1'=4,'pts_2'=2,'blk'=4] {'blk'}, dimensions={0} | all-to-all | bytes 1048576 | tf_op jit(solution)/shard_map/all_to_all | solution.py:26
  266.9 5.5 %all_to_all.36 = f32[2,1,16384]{2,1,0:T(1,128)S(1)} all-to-all(f32[2,1,16384]{2,1,0:T(1,128)S(1)} %reshape.36), channel_id=1, replica_groups=mesh['pts_0'=8,'pts_1'=4,'pts_2'=2,'blk'=4] {'pts_2'}, dimensions={0} | all-to-all | bytes 262144 | tf_op jit(solution)/shard_map/all_to_all | solution.py:26
  272.3 0.5 broadcast.16
  272.8 1.0 reduce.4
  274.2 18.2 %all_to_all.37 = f32[32,1,512]{2,1,0:T(1,128)S(1)} all-to-all(f32[32,1,512]{2,1,0:T(1,128)S(1)} %reshape.38), channel_id=1, replica_groups=mesh['pts_0'=8,'pts_1'=4,'pts_2'=2,'blk'=4] {'pts_0','pts_1'}, dimensions={0} | all-to-all | bytes 131072 | tf_op jit(solution)/shard_map/all_to_all | solution.py:34
  292.4 0.8 reduce.5
  293.5 12.0 %all_to_all.38 = f32[32,1,512]{2,1,0:T(1,128)S(1)} all-to-all(f32[32,1,512]{2,1,0:T(1,128)S(1)} %reshape.40), channel_id=1, replica_groups=mesh['pts_0'=8,'pts_1'=4,'pts_2'=2,'blk'=4] {'pts_0','pts_1'}, dimensions={0} | all-to-all | bytes 131072 | tf_op jit(solution)/shard_map/all_to_all | solution.py:45
  305.5 0.8 reduce.6
  306.6 6.6 %all_to_all.39 = f32[2,1,16384]{2,1,0:T(1,128)S(1)} all-to-all(f32[2,1,16384]{2,1,0:T(1,128)S(1)} %reshape.42), channel_id=1, replica_groups=mesh['pts_0'=8,'pts_1'=4,'pts_2'=2,'blk'=4] {'pts_2'}, dimensions={0} | all-to-all | bytes 262144 | tf_op jit(solution)/shard_map/all_to_all | solution.py:45
  313.2 1.0 reduce.7
  314.6 11.6 %all_to_all.40 = f32[4,512,64]{1,2,0:T(8,128)S(1)} all-to-all(f32[4,512,64]{1,2,0:T(8,128)S(1)} %broadcast_in_dim.33), channel_id=1, replica_groups=mesh['pts_0'=8,'pts_1'=4,'pts_2'=2,'blk'=4] {'blk'}, dimensions={0} | all-to-all | bytes 1048576 | tf_op jit(solution)/shard_map/all_to_all | solution.py:45
  326.2 6.3 %convolution_bitcast_fusion.1 = f32[512,64]{0,1:T(8,128)S(1)} fusion(f32[2048,64]{0,1:T(8,128)S(1)} %bitcast.76, f32[512,2048]{1,0:T(8,128)} %param.12), kind=kOutput, calls=%fused_computation.14 | convolution fusion | flops 805306368 | bytes 4849664 | tf_op jit(solution)/shard_map/dot_general | solution.py:103
  332.6 10.8 %all_to_all.41 = f32[4,512,64]{1,2,0:T(8,128)S(1)} all-to-all(f32[4,512,64]{1,2,0:T(8,128)S(1)} %broadcast_in_dim.34), channel_id=1, replica_groups=mesh['pts_0'=8,'pts_1'=4,'pts_2'=2,'blk'=4] {'blk'}, dimensions={0} | all-to-all | bytes 1048576 | tf_op jit(solution)/shard_map/all_to_all | solution.py:45
  343.7 0.8 select_n.49
  344.5 19.0 %convolution_add_fusion = f32[8192,64]{0,1:T(8,128)} fusion(f32[8192,64]{0,1:T(8,128)} %param.11, bf16[8192,2048]{1,0:T(8,128)(2,1)} %bitcast.71, bf16[2048,64]{0,1:T(8,128)(2,1)S(1)} %bitcast.82), kind=kOutput, calls=%fused_computation.11 | convolution fusion | flops 2148007936 | bytes 38010880 | tf_op jit(solution)/shard_map/nbs,bd->nsd/dot_general | solution.py:109
  (48 shorter events, 6.4 us)
Async XLA Ops:
  7.2 62.9 %all-gather.9.cloned.1.call-start = ((), (), s32[]{:S(2)}) async-start(), calls=%async_computation.7 | async-start | bytes 4718592 | tf_op jit(solution)/shard_map/all_gather | solution.py:15
  11.5 94.3 %all-gather.11.cloned.1.call-start = ((), (), s32[]{:S(2)}) async-start(), calls=%async_computation.8 | async-start | bytes 2621440 | tf_op jit(solution)/shard_map/all_gather | solution.py:15
  73.8 50.4 %all-gather.13.cloned.1.call-start = ((), (), s32[]{:S(2)}) async-start(), calls=%async_computation.9 | async-start | bytes 1572864 | tf_op jit(solution)/shard_map/all_gather | solution.py:15
  108.7 51.8 %all-gather.15.cloned.1.call-start = ((), (), s32[]{:S(2)}) async-start(), calls=%async_computation.10 | async-start | bytes 2621440 | tf_op jit(solution)/shard_map/all_gather | solution.py:15
  344.5 19.1 %copy-start = (f32[8192,64]{0,1:T(8,128)}, f32[8192,64]{0,1:T(8,128)S(1)}, u32[]{:S(2)}) copy-start(f32[8192,64]{0,1:T(8,128)S(1)} %select_n.49) | copy-start | bytes 6291460
Sparse Core Ops, SparseCore 0:
  11.7 58.3 all-gather.8
  73.9 31.8 all-gather.10
  108.8 15.3 all-gather.12
  126.7 33.7 all-gather.14
